TPU v7x, 256 devices: a whole 4x4x8 slice. The times are simulated.
256 devices in a mesh: blk: 8 (over z_lo, core), wide: 32 (over x, z_hi, y).
Axes of the slice: x: 4, y: 4, z: 8 (z_hi: 2, z_lo: 4; z = z_hi * 4 + z_lo), core: 2. Of those that a mesh axis runs over, the one named last changes fastest.
Arguments:
- surf_xyz: float32 [3, 131072], P(None, ('blk', 'wide')), may hold values from -5 to 5
- surf_disp: float32 [24, 131072], P(None, ('blk', 'wide')), may hold values from -12 to 12
- neighbours: int32 [4, 131072], P(None, ('blk', 'wide')), may hold values from 0 to 16383, as said below
- vol_xyz: float32 [3, 65536], P(None, ('blk', 'wide')), may hold values from -4 to 4
Outputs:
- displacement: float32 [24, 65536], P(None, ('blk', 'wide'))
Inputs may be any that keep to these rules, and one draw needn't show every extreme that they name: `neighbours`: column j names surface nodes of the same group of 16384 consecutive nodes as j, by their index within that group; every group is a renumbering of square patches of 16 x 16 nodes.
All inputs are finite; a program needn't handle non-finite values.
Results may differ from a plain program's by a relative error of at most 0.012.
The roundings to bfloat16 on the way count: a program that leaves them out, or rounds other values in their place, can miss the bound.
Values may be sent and summed in bfloat16 or wider, within the bound.
A program may use at most 64 MiB of HBM per device.

v0:
```python
import math
import jax
import jax.numpy as jnp
from jax import lax
from jax.sharding import PartitionSpec as P

tangent_floor = 0.04
core_radius = 0.04


def from_behind(shard, axis, by):
    peers = lax.axis_size(axis)
    return lax.ppermute(shard, axis, [(i, (i + by) % peers) for i in range(peers)])


def form_blocks(source_xyz, source_disp, links, node_xyz, node_disp):
    count = links.shape[1]
    cases = node_disp.shape[0] // 3
    tangent_one = jnp.take(source_xyz, links[0], axis=1) - jnp.take(source_xyz, links[1], axis=1)
    tangent_two = jnp.take(source_xyz, links[2], axis=1) - jnp.take(source_xyz, links[3], axis=1)
    change_one = (
        jnp.take(source_disp, links[0], axis=1) - jnp.take(source_disp, links[1], axis=1)
    ).reshape(cases, 3, count)
    change_two = (
        jnp.take(source_disp, links[2], axis=1) - jnp.take(source_disp, links[3], axis=1)
    ).reshape(cases, 3, count)
    length_one = (
        tangent_one[0] * tangent_one[0]
        + tangent_one[1] * tangent_one[1]
        + tangent_one[2] * tangent_one[2]
    )
    length_two = (
        tangent_two[0] * tangent_two[0]
        + tangent_two[1] * tangent_two[1]
        + tangent_two[2] * tangent_two[2]
    )
    scaled_one = tangent_one / (length_one + tangent_floor)
    scaled_two = tangent_two / (length_two + tangent_floor)
    linear = (
        change_one[:, :, None, :] * scaled_one[None, None, :, :]
        + change_two[:, :, None, :] * scaled_two[None, None, :, :]
    )
    moved = node_disp.reshape(cases, 3, count)
    offset = (
        linear[:, :, 0, :] * node_xyz[0]
        + linear[:, :, 1, :] * node_xyz[1]
        + linear[:, :, 2, :] * node_xyz[2]
    )
    blocks = jnp.concatenate([linear.reshape(cases, 9, count), moved - offset], axis=1)
    return blocks.reshape(cases * 12, count).astype(jnp.bfloat16)


def pair_weights(source_xyz, target_xyz):
    delta_x = source_xyz[0][:, None] - target_xyz[0][None, :]
    delta_y = source_xyz[1][:, None] - target_xyz[1][None, :]
    delta_z = source_xyz[2][:, None] - target_xyz[2][None, :]
    radius = delta_x * delta_x + delta_y * delta_y + delta_z * delta_z + core_radius
    return (1.0 / (radius * radius)).astype(jnp.bfloat16)


def finish(numerator, denominator, target_xyz):
    cases = numerator.shape[0] // 12
    count = numerator.shape[1]
    grouped = numerator.reshape(cases, 12, count)
    linear = grouped[:, :9].reshape(cases, 3, 3, count)
    moved = (
        linear[:, :, 0] * target_xyz[0]
        + linear[:, :, 1] * target_xyz[1]
        + linear[:, :, 2] * target_xyz[2]
        + grouped[:, 9:]
    )
    return (moved / denominator).reshape(cases * 3, count)


def accumulate(blocks, group_xyz, target_xyz, numerator, denominator):
    count = blocks.shape[1]
    width = math.gcd(1024, count)

    def one_piece(index, carry):
        partial_num, partial_den = carry
        start = index * width
        block_piece = lax.dynamic_slice_in_dim(blocks, start, width, 1)
        source_piece = lax.dynamic_slice_in_dim(group_xyz, start, width, 1)
        weights = pair_weights(source_piece, target_xyz)
        partial_num = partial_num + jnp.dot(
            block_piece, weights, preferred_element_type=jnp.float32
        )
        partial_den = partial_den + jnp.sum(weights.astype(jnp.float32), axis=0)
        return (partial_num, partial_den)

    return lax.fori_loop(0, count // width, one_piece, (numerator, denominator))


def on_device(surf_xyz, surf_disp, neighbours, vol_xyz):
    group_xyz, group_disp = (
        lax.all_gather(surf_xyz, "wide", axis=1, tiled=True),
        lax.all_gather(surf_disp, "wide", axis=1, tiled=True),
    )
    own_blocks = form_blocks(group_xyz, group_disp, neighbours, surf_xyz, surf_disp)
    blocks = lax.all_gather(own_blocks, "wide", axis=1, tiled=True)
    rows = blocks.shape[0]
    volume = vol_xyz.shape[1]
    groups = lax.axis_size("blk")
    visit_xyz = vol_xyz
    numerator = jnp.zeros((rows, volume), jnp.float32)
    denominator = jnp.zeros((volume,), jnp.float32)
    for step in range(groups):
        numerator, denominator = accumulate(blocks, group_xyz, visit_xyz, numerator, denominator)
        visit_xyz, numerator, denominator = from_behind(
            (visit_xyz, numerator, denominator), "blk", 1
        )
    return finish(numerator, denominator, vol_xyz)


def solution(mesh):
    in_specs = (
        P(None, ("blk", "wide")),
        P(None, ("blk", "wide")),
        P(None, ("blk", "wide")),
        P(None, ("blk", "wide")),
    )
    out_specs = P(None, ("blk", "wide"))
    return jax.shard_map(
        on_device, mesh=mesh, in_specs=in_specs, out_specs=out_specs, check_vma=False
    )
```

profile of v0, /device:TPU:2, one launch (start us, length us, event | category | flops | bytes accessed | tf_op | source)
XLA Modules:
  0.0 806.8 jit_solution(5151948245214430202)
XLA Ops:
  6.5 1.6 copy.76
  10.0 316.1 %all_gather.10 = f32[3,16384]{0,1:T(8,128)} all-gather(f32[3,512]{0,1:T(8,128)S(1)} %copy.80), channel_id=1, replica_groups=mesh['blk'=8,'wide'=32] {'wide'}, dimensions={1}, use_global_device_ids=true | all-gather | bytes 202752 | tf_op jit(solution)/shard_map/all_gather | solution.py:96
  326.1 4.4 gather_fusion.7
  330.6 4.4 gather_fusion.6
  335.3 4.4 gather_fusion.3
  339.8 4.4 gather_fusion.2
  344.5 4.4 gather_fusion.5
  349.0 4.4 gather_fusion.4
  353.7 4.4 gather_fusion.1
  358.2 4.4 gather_fusion
  363.9 5.5 copy.90
  369.3 97.1 %all-gather.5.cloned.1.call-done = bf16[96,16384]{1,0:T(8,128)(2,1)} async-done(((bf16[96,512]{1,0:T(8,128)(2,1)}), bf16[96,16384]{1,0:T(8,128)(2,1)}) %all-gather.5.cloned.1.call-update) | async-done | bytes 3145744 | tf_op jit(solution)/shard_map/all_gather | solution.py:100
  466.4 35.8 %while.128 = (s32[]{:T(128)}, f32[96,256]{1,0:T(8,128)S(1)}, f32[256]{0:T(256)S(1)}, bf16[96,16384]{1,0:T(8,128)(2,1)}, f32[3,16384]{1,0:T(4,128)S(1)}, /*index=...) while((s32[]{:T(128)}, f32[96,256]{1,0:T(8,128)S(1)}, ...), condition=%wide.region_2.5_spmd.clone, body=%wide.region_0.4_spmd.clone.sunk | while | flops 57196808 | bytes 458974 | solution.py:91
  471.5 1.6 convolution_add_fusion.23
  478.2 1.6 convolution_add_fusion.23
  484.9 1.6 convolution_add_fusion.23
  491.7 1.6 convolution_add_fusion.23
  503.2 5.0 collective-permute-done.2
  508.3 35.6 %while.121 = (s32[]{:T(128)}, f32[96,256]{1,0:T(8,128)S(1)}, f32[256]{0:T(256)S(1)}, bf16[96,16384]{1,0:T(8,128)(2,1)}, f32[3,16384]{1,0:T(4,128)S(1)}, /*index=...) while((s32[]{:T(128)}, f32[96,256]{1,0:T(8,128)S(1)}, ...), condition=%wide.region_5.8_spmd, body=%wide.region_3.7_spmd.sunk | while | flops 57171976 | bytes 458955 | solution.py:91
  544.3 5.5 collective-permute-done.5
  549.8 35.5 %while.122 = (s32[]{:T(128)}, f32[96,256]{1,0:T(8,128)S(1)}, f32[256]{0:T(256)S(1)}, bf16[96,16384]{1,0:T(8,128)(2,1)}, f32[3,16384]{1,0:T(4,128)S(1)}, /*index=...) while((s32[]{:T(128)}, f32[96,256]{1,0:T(8,128)S(1)}, ...), condition=%wide.region_8.11_spmd, body=%wide.region_6.10_spmd.sunk | while | flops 57171976 | bytes 458955 | solution.py:91
  585.7 5.7 collective-permute-done.8
  591.4 35.5 %while.123 = (s32[]{:T(128)}, f32[96,256]{1,0:T(8,128)S(1)}, f32[256]{0:T(256)S(1)}, bf16[96,16384]{1,0:T(8,128)(2,1)}, f32[3,16384]{1,0:T(4,128)S(1)}, /*index=...) while((s32[]{:T(128)}, f32[96,256]{1,0:T(8,128)S(1)}, ...), condition=%wide.region_11.14_spmd, body=%wide.region_9.13_spmd.sunk | while | flops 57171976 | bytes 458955 | solution.py:91
  627.2 5.7 collective-permute-done.11
  633.0 35.5 %while.124 = (s32[]{:T(128)}, f32[96,256]{1,0:T(8,128)S(1)}, f32[256]{0:T(256)S(1)}, bf16[96,16384]{1,0:T(8,128)(2,1)}, f32[3,16384]{1,0:T(4,128)S(1)}, /*index=...) while((s32[]{:T(128)}, f32[96,256]{1,0:T(8,128)S(1)}, ...), condition=%wide.region_14.17_spmd, body=%wide.region_12.16_spmd.sunk | while | flops 57171976 | bytes 458955 | solution.py:91
  668.8 5.7 collective-permute-done.14
  674.6 35.5 %while.125 = (s32[]{:T(128)}, f32[96,256]{1,0:T(8,128)S(1)}, f32[256]{0:T(256)S(1)}, bf16[96,16384]{1,0:T(8,128)(2,1)}, f32[3,16384]{1,0:T(4,128)S(1)}, /*index=...) while((s32[]{:T(128)}, f32[96,256]{1,0:T(8,128)S(1)}, ...), condition=%wide.region_17.20_spmd, body=%wide.region_15.19_spmd.sunk | while | flops 57171976 | bytes 458955 | solution.py:91
  710.6 5.5 collective-permute-done.17
  716.1 35.5 %while.126 = (s32[]{:T(128)}, f32[96,256]{1,0:T(8,128)S(1)}, f32[256]{0:T(256)S(1)}, bf16[96,16384]{1,0:T(8,128)(2,1)}, f32[3,16384]{1,0:T(4,128)S(1)}, /*index=...) while((s32[]{:T(128)}, f32[96,256]{1,0:T(8,128)S(1)}, ...), condition=%wide.region_20.23_spmd, body=%wide.region_18.22_spmd.sunk | while | flops 57171976 | bytes 458955 | solution.py:91
  752.0 5.7 collective-permute-done.20
  757.7 35.5 %while.127 = (s32[]{:T(128)}, f32[96,256]{1,0:T(8,128)S(1)}, f32[256]{0:T(256)S(1)}, bf16[96,16384]{1,0:T(8,128)(2,1)}, f32[3,16384]{1,0:T(4,128)S(1)}, /*index=...) while((s32[]{:T(128)}, f32[96,256]{1,0:T(8,128)S(1)}, ...), condition=%wide.region_23.26_spmd, body=%wide.region_21.25_spmd.sunk | while | flops 57171976 | bytes 458955 | solution.py:91
  793.5 5.7 collective-permute-done.21
  (735 shorter events, 281.0 us)
Async XLA Ops:
  6.5 338.0 %all-gather.3.cloned.1.call-start = ((), (), s32[]{:S(2)}) async-start(), calls=%async_computation | async-start | bytes 8650752 | tf_op jit(solution)/shard_map/all_gather | solution.py:97
  8.2 458.2 %all-gather.5.cloned.1.call-start = ((), (), s32[]{:S(2)}) async-start(), calls=%async_computation.1 | async-start | bytes 3244032 | tf_op jit(solution)/shard_map/all_gather | solution.py:100
  10.0 316.1 %copy-start = (f32[24,512]{1,0:T(8,128)S(1)}, f32[24,512]{1,0:T(8,128)}, u32[]{:S(2)}) copy-start(f32[24,512]{1,0:T(8,128)} %param.25) | copy-start | bytes 147460
  10.0 334.5 %copy-start.2 = (f32[3,512]{1,0:T(4,128)S(1)}, f32[3,512]{1,0:T(4,128)}, u32[]{:S(2)}) copy-start(f32[3,512]{1,0:T(4,128)} %param.24) | copy-start | bytes 18436
  363.8 102.6 %copy-start.1 = (f32[3,256]{1,0:T(4,128)S(1)}, f32[3,256]{1,0:T(4,128)}, u32[]{:S(2)}) copy-start(f32[3,256]{1,0:T(4,128)} %param.27) | copy-start | bytes 9220
  502.3 6.0 collective-permute-start
  502.3 5.9 collective-permute-start.2
  503.1 5.1 collective-permute-start.1
  543.8 6.0 collective-permute-start.3
  543.9 5.9 collective-permute-start.5
  544.0 5.8 collective-permute-start.4
  585.4 6.0 collective-permute-start.6
  585.5 5.9 collective-permute-start.8
  585.6 5.8 collective-permute-start.7
  627.0 6.0 collective-permute-start.9
  627.1 5.9 collective-permute-start.11
  627.2 5.8 collective-permute-start.10
  668.6 6.0 collective-permute-start.12
  668.6 5.9 collective-permute-start.14
  668.7 5.8 collective-permute-start.13
  710.1 6.0 collective-permute-start.15
  710.2 5.9 collective-permute-start.17
  710.5 5.6 collective-permute-start.16
  751.7 6.0 collective-permute-start.18
  751.8 5.9 collective-permute-start.20
  751.9 5.8 collective-permute-start.19
  793.3 5.9 collective-permute-start.21
  793.4 5.9 collective-permute-start.22
Sparse Core Ops, SparseCore 0:
  10.9 230.4 all-gather.2
  363.9 102.4 all-gather.4
where the time goes:
time: 811 us; the launch traced here: 807 us
  blocking collectives  316 us (39%)
  matrix products  201 us (25%)
  waiting for transfers between devices  142 us (18%)
  other arithmetic  66.2 us (8%)
  local copies, waits for them, and re-layouts  58.7 us (7%)
  between operations  14 us (2%)
    all_gather x1, blocking collectives, on_device(): lax.all_gather(surf_xyz, 'wide', axis=1, tiled=True)  316 us
    dot_general x128, matrix products, one_piece(): jnp.dot(block_piece, weights, preferred_element_type=jnp.float32)  201 us
    all_gather x1, waiting for transfers between devices, on_device(): blocks = lax.all_gather(own_blocks, 'wide', axis=1, tiled=True)  97.1 us
    reduce_sum x128, other arithmetic, one_piece(): partial_den = partial_den + jnp.sum(weights.astype(jnp.float32), axis=0)  64.1 us
    ppermute x23, waiting for transfers between devices, from_behind(): lax.ppermute(shard, axis, [(i, (i + by) % peers) for i in range(peers)])  44.8 us
  transfers between devices with their start and end apart: 25, of which 16 were waited for; matrix products, arithmetic and copies ran while one was open for 3% of the time, Pallas kernels for 0%

commit v1 on v0

--- a/solution.py
+++ b/solution.py
@@ -97,7 +97,9 @@
         lax.all_gather(surf_disp, "wide", axis=1, tiled=True),
     )
     own_blocks = form_blocks(group_xyz, group_disp, neighbours, surf_xyz, surf_disp)
-    blocks = lax.all_gather(own_blocks, "wide", axis=1, tiled=True)
+    blocks = jnp.concatenate(
+        lax.all_to_all(jnp.stack([own_blocks] * lax.axis_size("wide")), "wide", 0, 0), axis=1
+    )
     rows = blocks.shape[0]
     volume = vol_xyz.shape[1]
     groups = lax.axis_size("blk")

time: 811 us -> 786 us (0.969)
  waiting for transfers between devices: 142 us -> 79.6 us
  starting transfers between devices: 3.08 us -> 38.6 us
    all_gather x1 -> x0, waiting for transfers between devices: 97.1 us -> none  [on_device(): blocks = lax.all_gather(own_blocks, 'wide', axis=1, tiled=True)]
    all_to_all x0 -> x1, waiting for transfers between devices: none -> 30.6 us  [on_device(): lax.all_to_all(jnp.stack([own_blocks] * lax.axis_size('wide')), 'wide', 0...]
    ppermute x23, starting transfers between devices: 3.04 us -> 33.4 us  [from_behind(): lax.ppermute(shard, axis, [(i, (i + by) % peers) for i in range(peers)])]
where the time goes in v1:
time: 786 us; the launch traced here: 780 us
  blocking collectives  313 us (40%)
  matrix products  201 us (26%)
  waiting for transfers between devices  79.6 us (10%)
  other arithmetic  66.2 us (8%)
  local copies, waits for them, and re-layouts  62 us (8%)
  starting transfers between devices  38.6 us (5%)
  between operations  14 us (2%)
    all_gather x1, blocking collectives, on_device(): lax.all_gather(surf_xyz, 'wide', axis=1, tiled=True)  313 us
    dot_general x128, matrix products, one_piece(): jnp.dot(block_piece, weights, preferred_element_type=jnp.float32)  201 us
    reduce_sum x128, other arithmetic, one_piece(): partial_den = partial_den + jnp.sum(weights.astype(jnp.float32), axis=0)  64.1 us
    ppermute x23, waiting for transfers between devices, from_behind(): lax.ppermute(shard, axis, [(i, (i + by) % peers) for i in range(peers)])  49 us
    ppermute x23, starting transfers between devices, from_behind(): lax.ppermute(shard, axis, [(i, (i + by) % peers) for i in range(peers)])  33.4 us
    all_to_all x1, waiting for transfers between devices, on_device(): lax.all_to_all(jnp.stack([own_blocks] * lax.axis_size('wide')), 'wide', 0...  30.6 us
  transfers between devices with their start and end apart: 25, of which 16 were waited for; matrix products, arithmetic and copies ran while one was open for 3% of the time, Pallas kernels for 0%

profile of v1, /device:TPU:2, one launch (start us, length us, event | category | flops | bytes accessed | tf_op | source)
XLA Modules:
  0.0 780.2 jit_solution(4097525712431516913)
XLA Ops:
  9.9 313.0 %all_gather.7 = f32[3,16384]{0,1:T(8,128)} all-gather(f32[3,512]{0,1:T(8,128)S(1)} %copy.134), channel_id=1, replica_groups=mesh['blk'=8,'wide'=32] {'wide'}, dimensions={1}, use_global_device_ids=true | all-gather | bytes 202752 | tf_op jit(solution)/shard_map/all_gather | solution.py:96
  322.9 4.4 gather_fusion.7
  327.5 4.4 gather_fusion.6
  332.2 4.4 gather_fusion.3
  336.7 4.4 gather_fusion.2
  341.4 4.4 gather_fusion.5
  345.8 4.4 gather_fusion.4
  350.6 4.4 gather_fusion.1
  355.0 4.4 gather_fusion
  362.0 5.2 all-to-all-start
  367.2 5.5 copy.145
  372.7 30.6 %all-to-all-done = bf16[32,96,512]{2,1,0:T(8,128)(2,1)S(1)} async-done(((bf16[32,96,512]{2,1,0:T(8,128)(2,1)}), bf16[32,96,512]{2,1,0:T(8,128)(2,1)S(1)}, u32[]{:S(2)}, u32[]{:S(2)}) %all-to-all-start) | async-done | bytes 3145760 | tf_op jit(solution)/shard_map/all_to_all | solution.py:101
  405.2 35.8 %while.128 = (s32[]{:T(128)}, f32[96,256]{1,0:T(8,128)S(1)}, f32[256]{0:T(256)S(1)}, bf16[96,16384]{1,0:T(8,128)(2,1)}, f32[3,16384]{1,0:T(4,128)S(1)}, /*index=...) while((s32[]{:T(128)}, f32[96,256]{1,0:T(8,128)S(1)}, ...), condition=%wide.region_2.5_spmd.clone, body=%wide.region_0.4_spmd.clone.sunk | while | flops 57196808 | bytes 458974 | solution.py:91
  441.2 22.8 %collective-permute-start.2 = (f32[3,256]{1,0:T(4,128)S(1)}, f32[3,256]{1,0:T(4,128)S(1)}, u32[]{:S(2)}, u32[]{:S(2)}) collective-permute-start(f32[3,256]{1,0:T(4,128)S(1)} %get-tuple-element.2075), channel_id=1, source_target_pairs={{0,32},{32,64},{64,96},{96,128},{128,160},{160,192},{192,224},{224... | collective-permute-start | bytes 9224 | tf_op jit(solution)/shard_map/ppermute | solution.py:13
  464.1 10.0 %collective-permute-done.2 = f32[3,256]{1,0:T(4,128)S(1)} collective-permute-done((f32[3,256]{1,0:T(4,128)S(1)}, f32[3,256]{1,0:T(4,128)S(1)}, u32[]{:S(2)}, u32[]{:S(2)}) %collective-permute-start.2) | collective-permute-done | bytes 3104 | tf_op jit(solution)/shard_map/ppermute | solution.py:13
  474.1 35.5 %while.121 = (s32[]{:T(128)}, f32[96,256]{1,0:T(8,128)S(1)}, f32[256]{0:T(256)S(1)}, bf16[96,16384]{1,0:T(8,128)(2,1)}, f32[3,16384]{1,0:T(4,128)S(1)}, /*index=...) while((s32[]{:T(128)}, f32[96,256]{1,0:T(8,128)S(1)}, ...), condition=%wide.region_5.8_spmd, body=%wide.region_3.7_spmd.sunk | while | flops 57171976 | bytes 458955 | solution.py:91
  509.7 6.5 collective-permute-start.3
  516.2 2.3 collective-permute-start.5
  518.5 2.5 collective-permute-done.5
  521.0 2.3 collective-permute-done.4
  523.2 35.6 %while.122 = (s32[]{:T(128)}, f32[96,256]{1,0:T(8,128)S(1)}, f32[256]{0:T(256)S(1)}, bf16[96,16384]{1,0:T(8,128)(2,1)}, f32[3,16384]{1,0:T(4,128)S(1)}, /*index=...) while((s32[]{:T(128)}, f32[96,256]{1,0:T(8,128)S(1)}, ...), condition=%wide.region_8.11_spmd, body=%wide.region_6.10_spmd.sunk | while | flops 57171976 | bytes 458955 | solution.py:91
  559.1 5.7 collective-permute-done.8
  564.8 35.5 %while.123 = (s32[]{:T(128)}, f32[96,256]{1,0:T(8,128)S(1)}, f32[256]{0:T(256)S(1)}, bf16[96,16384]{1,0:T(8,128)(2,1)}, f32[3,16384]{1,0:T(4,128)S(1)}, /*index=...) while((s32[]{:T(128)}, f32[96,256]{1,0:T(8,128)S(1)}, ...), condition=%wide.region_11.14_spmd, body=%wide.region_9.13_spmd.sunk | while | flops 57171976 | bytes 458955 | solution.py:91
  600.6 5.7 collective-permute-done.11
  606.4 35.5 %while.124 = (s32[]{:T(128)}, f32[96,256]{1,0:T(8,128)S(1)}, f32[256]{0:T(256)S(1)}, bf16[96,16384]{1,0:T(8,128)(2,1)}, f32[3,16384]{1,0:T(4,128)S(1)}, /*index=...) while((s32[]{:T(128)}, f32[96,256]{1,0:T(8,128)S(1)}, ...), condition=%wide.region_14.17_spmd, body=%wide.region_12.16_spmd.sunk | while | flops 57171976 | bytes 458955 | solution.py:91
  642.2 5.7 collective-permute-done.14
  648.0 35.5 %while.125 = (s32[]{:T(128)}, f32[96,256]{1,0:T(8,128)S(1)}, f32[256]{0:T(256)S(1)}, bf16[96,16384]{1,0:T(8,128)(2,1)}, f32[3,16384]{1,0:T(4,128)S(1)}, /*index=...) while((s32[]{:T(128)}, f32[96,256]{1,0:T(8,128)S(1)}, ...), condition=%wide.region_17.20_spmd, body=%wide.region_15.19_spmd.sunk | while | flops 57171976 | bytes 458955 | solution.py:91
  684.0 5.5 collective-permute-done.17
  689.5 35.5 %while.126 = (s32[]{:T(128)}, f32[96,256]{1,0:T(8,128)S(1)}, f32[256]{0:T(256)S(1)}, bf16[96,16384]{1,0:T(8,128)(2,1)}, f32[3,16384]{1,0:T(4,128)S(1)}, /*index=...) while((s32[]{:T(128)}, f32[96,256]{1,0:T(8,128)S(1)}, ...), condition=%wide.region_20.23_spmd, body=%wide.region_18.22_spmd.sunk | while | flops 57171976 | bytes 458955 | solution.py:91
  725.4 5.7 collective-permute-done.20
  731.1 35.5 %while.127 = (s32[]{:T(128)}, f32[96,256]{1,0:T(8,128)S(1)}, f32[256]{0:T(256)S(1)}, bf16[96,16384]{1,0:T(8,128)(2,1)}, f32[3,16384]{1,0:T(4,128)S(1)}, /*index=...) while((s32[]{:T(128)}, f32[96,256]{1,0:T(8,128)S(1)}, ...), condition=%wide.region_23.26_spmd, body=%wide.region_21.25_spmd.sunk | while | flops 57171976 | bytes 458955 | solution.py:91
  766.9 5.7 collective-permute-done.21
  (736 shorter events, 291.0 us)
Async XLA Ops:
  6.5 334.9 %all-gather.2.cloned.1.call-start = ((), (), s32[]{:S(2)}) async-start(), calls=%async_computation.1 | async-start | bytes 8650752 | tf_op jit(solution)/shard_map/all_gather | solution.py:97
  9.9 313.0 %copy-start = (f32[24,512]{1,0:T(8,128)S(1)}, f32[24,512]{1,0:T(8,128)}, u32[]{:S(2)}) copy-start(f32[24,512]{1,0:T(8,128)} %param.25) | copy-start | bytes 147460
  9.9 331.4 %copy-start.2 = (f32[3,512]{1,0:T(4,128)S(1)}, f32[3,512]{1,0:T(4,128)}, u32[]{:S(2)}) copy-start(f32[3,512]{1,0:T(4,128)} %param.24) | copy-start | bytes 18436
  362.0 41.2 %all-to-all-start = ((bf16[32,96,512]{2,1,0:T(8,128)(2,1)}), bf16[32,96,512]{2,1,0:T(8,128)(2,1)S(1)}, u32[]{:S(2)}, u32[]{:S(2)}) async-start(bf16[32,96,512]{2,1,0:T(8,128)(2,1)} %stack.2), calls=%async_computation | async-start | bytes 6291456 | tf_op jit(solution)/shard_map/all_to_all | solution.py:101
  403.3 2.0 copy-start.1
  441.1 33.1 %collective-permute-start = (f32[96,256]{1,0:T(8,128)S(1)}, f32[96,256]{1,0:T(8,128)S(1)}, u32[]{:S(2)}, u32[]{:S(2)}) collective-permute-start(f32[96,256]{1,0:T(8,128)S(1)} %get-tuple-element.887), channel_id=1, source_target_pairs={{0,32},{32,64},{64,96},{96,128},{128,160},{160,192},{192,224},{224... | collective-permute-start | bytes 294920 | tf_op jit(solution)/shard_map/ppermute | solution.py:13
  441.2 32.9 %collective-permute-start.2 = (f32[3,256]{1,0:T(4,128)S(1)}, f32[3,256]{1,0:T(4,128)S(1)}, u32[]{:S(2)}, u32[]{:S(2)}) collective-permute-start(f32[3,256]{1,0:T(4,128)S(1)} %get-tuple-element.2075), channel_id=1, source_target_pairs={{0,32},{32,64},{64,96},{96,128},{128,160},{160,192},{192,224},{224... | collective-permute-start | bytes 9224 | tf_op jit(solution)/shard_map/ppermute | solution.py:13
  464.0 10.2 %collective-permute-start.1 = (f32[256]{0:T(256)S(1)}, f32[256]{0:T(256)S(1)}, u32[]{:S(2)}, u32[]{:S(2)}) collective-permute-start(f32[256]{0:T(256)S(1)} %get-tuple-element.888), channel_id=1, source_target_pairs={{0,32},{32,64},{64,96},{96,128},{128,160},{160,192},{192,224},{224... | collective-permute-start | bytes 3080 | tf_op jit(solution)/shard_map/ppermute | solution.py:13
  509.7 13.5 %collective-permute-start.3 = (f32[96,256]{1,0:T(8,128)S(1)}, f32[96,256]{1,0:T(8,128)S(1)}, u32[]{:S(2)}, u32[]{:S(2)}) collective-permute-start(f32[96,256]{1,0:T(8,128)S(1)} %get-tuple-element.889), channel_id=1, source_target_pairs={{0,32},{32,64},{64,96},{96,128},{128,160},{160,192},{192,224},{224... | collective-permute-start | bytes 294920 | tf_op jit(solution)/shard_map/ppermute | solution.py:13
  516.2 4.8 collective-permute-start.5
  518.4 4.8 collective-permute-start.4
  558.8 6.0 collective-permute-start.6
  558.9 5.9 collective-permute-start.8
  559.0 5.8 collective-permute-start.7
  600.4 6.0 collective-permute-start.9
  600.5 5.9 collective-permute-start.11
  600.6 5.8 collective-permute-start.10
  641.9 6.0 collective-permute-start.12
  642.0 5.9 collective-permute-start.14
  642.1 5.8 collective-permute-start.13
  683.5 6.0 collective-permute-start.15
  683.6 5.9 collective-permute-start.17
  683.9 5.6 collective-permute-start.16
  725.1 6.0 collective-permute-start.18
  725.2 5.9 collective-permute-start.20
  725.3 5.8 collective-permute-start.19
  766.7 5.9 collective-permute-start.21
  766.8 5.9 collective-permute-start.22
Sparse Core Ops, SparseCore 0:
  10.9 223.8 all-gather.1
